TPU v7x, 32 devices: a whole 2x2x4 slice. The times are simulated.
32 devices in a mesh: groups: 2 (over x), ctx: 8 (over z, y), head: 2 (over core).
Axes of the slice: x: 2, y: 2, z: 4, core: 2. Of those that a mesh axis runs over, the one named last changes fastest.
Arguments:
- queries: bfloat16 [2, 256, 64, 128], P('groups', 'ctx', 'head'), parts along dimension 0, may hold values from -400 to 400
- new_keys: bfloat16 [2, 256, 8, 128], P('groups', 'ctx', 'head'), parts along dimension 0, may hold values from -5 to 5
- new_values: bfloat16 [2, 256, 8, 128], P('groups', 'ctx', 'head'), parts along dimension 0, may hold values from -6 to 6
- history_keys: bfloat16 [2, 8192, 8, 128], P('groups', 'ctx', 'head'), parts along dimension 0, may hold values from -6 to 6
- history_values: bfloat16 [2, 8192, 8, 128], P('groups', 'ctx', 'head'), parts along dimension 0, may hold values from -6 to 6
- block_mask: int32 [2, 2, 64], P('groups', None, 'ctx'), parts along dimension 0, may hold values from 0 to 1, as said below
Outputs:
- attended: bfloat16 [2, 256, 64, 128], P('groups', 'ctx', 'head'), parts along dimension 0
There are 2 independent parts, one for each index of `groups`. A program takes and returns all parts, laid end to end along the dimension named above; each array names one. Nothing has to cross between parts.
Inputs may be any that keep to these rules, and one draw needn't show every extreme that they name: `block_mask`: 0 or 1 for each pair of a block of 128 new tokens and a block of 128 history positions of the same session.
All inputs are finite; a program needn't handle non-finite values.
Results may differ from a plain program's by a relative error of at most 0.0013.
Values may be sent and summed in bfloat16 or wider, within the bound.
A program may use at most 64 MiB of HBM per device.

v0:
```python
import math
import jax
import jax.numpy as jnp
from jax import lax
from jax.sharding import PartitionSpec as P

BLK = 128
NEG = -1e30


def attend(query_rows, keys_t, values_t, visible):
    sess, rows, local_heads, head_size = query_rows.shape
    kv_local = keys_t.shape[0]
    group = local_heads // kv_local
    grouped = jnp.moveaxis(query_rows.reshape(sess, rows, kv_local, group, head_size), 2, 0)
    scale = 1.0 / math.sqrt(head_size)
    seen = visible[:, None]

    def one_head(operands):
        q_head, k_head, v_head = operands
        scores = (
            jnp.einsum("srgd,scd->sgrc", q_head, k_head, preferred_element_type=jnp.float32) * scale
        )
        masked = jnp.where(seen, scores, NEG)
        peak = jnp.max(masked, axis=-1)
        expo = jnp.where(seen, jnp.exp(masked - peak[..., None]), 0.0)
        total = jnp.sum(expo, axis=-1)
        summed = jnp.einsum(
            "sgrc,scd->sgrd", expo, v_head.astype(jnp.float32), precision=lax.Precision.HIGHEST
        )
        return (peak, total, summed)

    peak, total, summed = lax.map(one_head, (grouped, keys_t, values_t))
    peak = jnp.transpose(peak, (1, 3, 0, 2)).reshape(sess, rows, local_heads)
    total = jnp.transpose(total, (1, 3, 0, 2)).reshape(sess, rows, local_heads)
    summed = jnp.transpose(summed, (1, 3, 0, 2, 4)).reshape(sess, rows, local_heads, head_size)
    return (peak, total, summed)


def per_device(queries, new_keys, new_values, history_keys, history_values, block_mask):
    sess, own, local_heads, head_size = queries.shape
    first = lax.axis_index("ctx") * own
    qblocks = block_mask.shape[1]
    own_ids = first + lax.iota(jnp.int32, own)
    mask_float = block_mask.astype(jnp.float32)
    keys_t = jnp.moveaxis(history_keys, 2, 0)
    values_t = jnp.moveaxis(history_values, 2, 0)
    piece = lax.all_gather(queries, "ctx", axis=1, tiled=True)
    rows = piece.shape[1]
    row_ids = lax.iota(jnp.int32, rows)
    onehot = (row_ids[:, None] // BLK == lax.iota(jnp.int32, qblocks)[None, :]).astype(jnp.float32)
    live = jnp.einsum("rq,sqb->srb", onehot, mask_float)
    visible = jnp.repeat(live, BLK, axis=2) > 0.5
    peak, total, summed = attend(piece, keys_t, values_t, visible)
    peak_all = peak
    total_all = total
    summed_all = summed
    peaks, totals, sums = (
        lax.all_to_all(peak_all[None], "ctx", split_axis=2, concat_axis=0, tiled=True),
        lax.all_to_all(total_all[None], "ctx", split_axis=2, concat_axis=0, tiled=True),
        lax.all_to_all(summed_all[None], "ctx", split_axis=2, concat_axis=0, tiled=True),
    )
    hist_top = jnp.max(peaks, axis=0)
    factor = jnp.exp(peaks - hist_top[None])
    hist_total = jnp.sum(totals * factor, axis=0)
    hist_sum = jnp.sum(sums * factor[..., None], axis=0)
    key_piece = lax.all_gather(new_keys, "ctx", axis=1, tiled=True)
    value_piece = lax.all_gather(new_values, "ctx", axis=1, tiled=True)
    cols = key_piece.shape[1]
    causal = lax.iota(jnp.int32, cols)[None, :] <= own_ids[:, None]
    visible = causal[None]
    peak, total, summed = attend(
        queries, jnp.moveaxis(key_piece, 2, 0), jnp.moveaxis(value_piece, 2, 0), visible
    )
    old_peak = jnp.full((sess, own, local_heads), NEG, jnp.float32)
    top = jnp.maximum(old_peak, peak)
    fresh = jnp.exp(peak - top)
    new_top = top
    new_total = total * fresh
    new_sum = summed * fresh[..., None]
    top = jnp.maximum(hist_top, new_top)
    old_scale = jnp.exp(hist_top - top)
    new_scale = jnp.exp(new_top - top)
    numer = hist_sum * old_scale[..., None] + new_sum * new_scale[..., None]
    denom = hist_total * old_scale + new_total * new_scale
    return (numer / denom[..., None]).astype(jnp.bfloat16)


def solution(mesh):
    placed = (
        P("groups", "ctx", "head", None),
        P("groups", "ctx", "head", None),
        P("groups", "ctx", "head", None),
        P("groups", "ctx", "head", None),
        P("groups", "ctx", "head", None),
        P("groups", None, "ctx"),
    )
    return jax.shard_map(
        per_device,
        mesh=mesh,
        in_specs=placed,
        out_specs=P("groups", "ctx", "head", None),
        check_vma=False,
    )
```

profile of v0, /device:TPU:0, one launch (start us, length us, event | category | flops | bytes accessed | tf_op | source)
XLA Modules:
  0.0 305.4 jit_solution(13688922537271445588)
XLA Ops:
  6.5 0.7 all-gather.2.cloned.1.call-update
  7.3 0.9 convolution_compare_fusion
  8.2 2.8 copy_bitcast_fusion.2
  11.0 50.3 %all-gather.2.cloned.1.call-done = bf16[1,256,32,128]{3,2,0,1:T(8,128)(2,1)} async-done(((bf16[1,32,32,128]{3,2,0,1:T(8,128)(2,1)}), bf16[1,256,32,128]{3,2,0,1:T(8,128)(2,1)}) %all-gather.2.cloned.1.call-update) | async-done | bytes 2097168 | tf_op jit(solution)/shard_map/all_gather | solution.py:48
  61.3 2.4 copy.68
  63.7 52.7 %while.30 = (s32[]{:T(128)}, f32[4,1,8,256]{3,2,1,0:T(8,128)S(1)}, f32[4,1,8,256]{3,2,1,0:T(8,128)S(1)}, f32[4,1,8,256,128]{4,3,2,1,0:T(8,128)}, bf16[4,1,1024,1...) while((s32[]{:T(128)}, f32[4,1,8,256]{3,2,1,0:T(8,128)S(1)}, ...), condition=%wide.region_3.4_spmd.clone, body=%wide.region_0.3_spmd.clone.sunk | while | flops 3783258112 | bytes 28381280 | solution.py:33
  63.8 1.4 fusion.77
  65.2 9.6 %fusion.79 = f32[4,1,8,256,128]{4,3,2,1,0:T(8,128)} fusion(f32[4,1,8,256,128]{4,3,2,1,0:T(8,128)} %get-tuple-element.309, s32[]{:T(128)} %get-tuple-element.306, f32[1024,256,8]{1,0,2:T(8,128)S(1)} %get-tuple-element.281, f32[8,256]{1,0:T(8,128)S(1)} %get-tuple-element.282, pred[256,1024]{0,1:T(8,128)(4,1)S(1)} %bitcast.191, ...), kind=kOutput, calls=%fused_computation.14.clone.1 | convolution fusion | flops 3229614080 | bytes 9970688 | tf_op jit(solution)/shard_map/while/body/eval_jaxpr/sgrc,scd->sgrd/dot_general | solution.py:28
  74.8 2.0 fusion.78
  77.0 1.4 fusion.77
  78.4 9.7 %fusion.79 = f32[4,1,8,256,128]{4,3,2,1,0:T(8,128)} fusion(f32[4,1,8,256,128]{4,3,2,1,0:T(8,128)} %get-tuple-element.309, s32[]{:T(128)} %get-tuple-element.306, f32[1024,256,8]{1,0,2:T(8,128)S(1)} %get-tuple-element.281, f32[8,256]{1,0:T(8,128)S(1)} %get-tuple-element.282, pred[256,1024]{0,1:T(8,128)(4,1)S(1)} %bitcast.191, ...), kind=kOutput, calls=%fused_computation.14.clone.1 | convolution fusion | flops 3229614080 | bytes 9970688 | tf_op jit(solution)/shard_map/while/body/eval_jaxpr/sgrc,scd->sgrd/dot_general | solution.py:28
  88.0 2.0 fusion.78
  90.2 1.4 fusion.77
  91.6 9.7 %fusion.79 = f32[4,1,8,256,128]{4,3,2,1,0:T(8,128)} fusion(f32[4,1,8,256,128]{4,3,2,1,0:T(8,128)} %get-tuple-element.309, s32[]{:T(128)} %get-tuple-element.306, f32[1024,256,8]{1,0,2:T(8,128)S(1)} %get-tuple-element.281, f32[8,256]{1,0:T(8,128)S(1)} %get-tuple-element.282, pred[256,1024]{0,1:T(8,128)(4,1)S(1)} %bitcast.191, ...), kind=kOutput, calls=%fused_computation.14.clone.1 | convolution fusion | flops 3229614080 | bytes 9970688 | tf_op jit(solution)/shard_map/while/body/eval_jaxpr/sgrc,scd->sgrd/dot_general | solution.py:28
  101.2 2.0 fusion.78
  103.4 1.4 fusion.77
  104.8 9.6 %fusion.79 = f32[4,1,8,256,128]{4,3,2,1,0:T(8,128)} fusion(f32[4,1,8,256,128]{4,3,2,1,0:T(8,128)} %get-tuple-element.309, s32[]{:T(128)} %get-tuple-element.306, f32[1024,256,8]{1,0,2:T(8,128)S(1)} %get-tuple-element.281, f32[8,256]{1,0:T(8,128)S(1)} %get-tuple-element.282, pred[256,1024]{0,1:T(8,128)(4,1)S(1)} %bitcast.191, ...), kind=kOutput, calls=%fused_computation.14.clone.1 | convolution fusion | flops 3229614080 | bytes 9970688 | tf_op jit(solution)/shard_map/while/body/eval_jaxpr/sgrc,scd->sgrd/dot_general | solution.py:28
  114.4 2.0 fusion.78
  117.1 0.9 reduce.7
  118.0 0.7 reshape.378
  118.8 3.5 %all-to-all-start.1 = ((f32[8,1,1024]{2,1,0:T(1,128)}), f32[8,1,1024]{2,1,0:T(1,128)S(1)}, u32[]{:S(2)}, u32[]{:S(2)}) async-start(f32[8,1,1024]{2,1,0:T(1,128)} %reshape.378), calls=%async_computation.1 | async-start | bytes 65536 | tf_op jit(solution)/shard_map/all_to_all | solution.py:59
  122.4 0.9 reduce.9
  123.4 0.7 reshape.380
  124.1 4.9 %all-to-all-done.1 = f32[8,1,1024]{2,1,0:T(1,128)S(1)} async-done(((f32[8,1,1024]{2,1,0:T(1,128)}), f32[8,1,1024]{2,1,0:T(1,128)S(1)}, u32[]{:S(2)}, u32[]{:S(2)}) %all-to-all-start.1) | async-done | bytes 32800 | tf_op jit(solution)/shard_map/all_to_all | solution.py:59
  128.9 3.3 %all-to-all-start.2 = ((f32[8,1,1024]{2,1,0:T(1,128)}), f32[8,1,1024]{2,1,0:T(1,128)S(1)}, u32[]{:S(2)}, u32[]{:S(2)}) async-start(f32[8,1,1024]{2,1,0:T(1,128)} %reshape.380), calls=%async_computation.2 | async-start | bytes 65536 | tf_op jit(solution)/shard_map/all_to_all | solution.py:60
  132.3 6.6 %copy.67 = f32[1,256,4,8,128]{4,3,2,1,0:T(8,128)} copy(f32[1,256,4,8,128]{4,1,3,0,2:T(8,128)} %bitcast.195) | data formatting | bytes 8388608 | tf_op jit(solution)/shard_map/transpose | solution.py:36
  138.9 5.9 %all-to-all-start = ((f32[1,1,256,32,128]{4,3,1,0,2:T(8,128)}), f32[1,1,256,32,128]{4,3,1,0,2:T(8,128)}, u32[]{:S(2)}, u32[]{:S(2)}) async-start(f32[1,1,256,32,128]{4,3,1,0,2:T(8,128)} %bitcast.193), calls=%async_computation | async-start | bytes 8388608 | tf_op jit(solution)/shard_map/all_to_all | solution.py:61
  145.0 111.1 %all_gather.10 = bf16[1,256,4,128]{3,1,0,2:T(8,128)(2,1)S(1)} all-gather(bf16[1,32,4,128]{3,1,0,2:T(8,128)(2,1)S(1)} %copy.50), channel_id=1, replica_groups=mesh['groups'=2,'ctx'=8,'head'=2] {'ctx'}, dimensions={1}, use_global_device_ids=true | all-gather | bytes 294912 | tf_op jit(solution)/shard_map/all_gather | solution.py:67
  256.1 30.9 %all_gather.11 = bf16[1,256,4,128]{3,1,0,2:T(8,128)(2,1)S(1)} all-gather(bf16[1,32,4,128]{3,1,0,2:T(8,128)(2,1)S(1)} %copy.52), channel_id=1, replica_groups=mesh['groups'=2,'ctx'=8,'head'=2] {'ctx'}, dimensions={1}, use_global_device_ids=true | all-gather | bytes 294912 | tf_op jit(solution)/shard_map/all_gather | solution.py:68
  287.0 3.7 %while.31 = (s32[]{:T(128)}, f32[4,1,8,32]{3,2,1,0:T(8,128)S(1)}, f32[4,1,8,32]{3,2,1,0:T(8,128)S(1)}, f32[4,1,8,32,128]{4,3,2,1,0:T(8,128)S(1)}, bf16[4,1,256,1...) while((s32[]{:T(128)}, f32[4,1,8,32]{3,2,1,0:T(8,128)S(1)}, ...), condition=%wide.region_9.10_spmd.clone, body=%wide.region_6.9_spmd.clone.sunk | while | flops 117972480 | bytes 1172705 | solution.py:33
  293.2 3.9 %fusion.49 = f32[32,32,128]{2,0,1:T(8,128)S(1)} fusion(f32[8,1,32,32,128]{4,3,2,0,1:T(8,128)} %bitcast.8, f32[8,32,32]{1,0,2:T(8,128)S(1)} %copy.48), kind=kLoop, calls=%fused_computation.54 | loop fusion | flops 1966080 | bytes 4751360 | tf_op jit(solution)/shard_map/reduce_sum | solution.py:66
  297.8 0.8 copy.57
  (64 shorter events, 7.7 us)
Async XLA Ops:
  6.5 54.8 %all-gather.2.cloned.1.call-start = ((), (), s32[]{:S(2)}) async-start(), calls=%async_computation.3 | async-start | bytes 2359296 | tf_op jit(solution)/shard_map/all_gather | solution.py:48
  118.8 10.2 %all-to-all-start.1 = ((f32[8,1,1024]{2,1,0:T(1,128)}), f32[8,1,1024]{2,1,0:T(1,128)S(1)}, u32[]{:S(2)}, u32[]{:S(2)}) async-start(f32[8,1,1024]{2,1,0:T(1,128)} %reshape.378), calls=%async_computation.1 | async-start | bytes 65536 | tf_op jit(solution)/shard_map/all_to_all | solution.py:59
  128.9 10.0 %all-to-all-start.2 = ((f32[8,1,1024]{2,1,0:T(1,128)}), f32[8,1,1024]{2,1,0:T(1,128)S(1)}, u32[]{:S(2)}, u32[]{:S(2)}) async-start(f32[8,1,1024]{2,1,0:T(1,128)} %reshape.380), calls=%async_computation.2 | async-start | bytes 65536 | tf_op jit(solution)/shard_map/all_to_all | solution.py:60
  132.3 12.5 %copy-start = (bf16[1,32,32,128]{3,2,1,0:T(8,128)(2,1)S(1)}, bf16[1,32,32,128]{3,2,1,0:T(8,128)(2,1)}, u32[]{:S(2)}) copy-start(bf16[1,32,32,128]{3,2,1,0:T(8,128)(2,1)} %param.10) | copy-start | bytes 786436
  132.3 12.7 %copy-start.1 = (bf16[1,32,4,128]{3,2,1,0:T(4,128)(2,1)S(1)}, bf16[1,32,4,128]{3,2,1,0:T(4,128)(2,1)}, u32[]{:S(2)}) copy-start(bf16[1,32,4,128]{3,2,1,0:T(4,128)(2,1)} %param.11) | copy-start | bytes 98308
  132.3 12.7 %copy-start.2 = (bf16[1,32,4,128]{3,2,1,0:T(4,128)(2,1)S(1)}, bf16[1,32,4,128]{3,2,1,0:T(4,128)(2,1)}, u32[]{:S(2)}) copy-start(bf16[1,32,4,128]{3,2,1,0:T(4,128)(2,1)} %param.12) | copy-start | bytes 98308
  138.9 154.3 %all-to-all-start = ((f32[1,1,256,32,128]{4,3,1,0,2:T(8,128)}), f32[1,1,256,32,128]{4,3,1,0,2:T(8,128)}, u32[]{:S(2)}, u32[]{:S(2)}) async-start(f32[1,1,256,32,128]{4,3,1,0,2:T(8,128)} %bitcast.193), calls=%async_computation | async-start | bytes 8388608 | tf_op jit(solution)/shard_map/all_to_all | solution.py:61
Sparse Core Ops, SparseCore 0:
  9.5 51.8 all-gather.1
where the time goes:
time: 306 us; the launch traced here: 305 us
  blocking collectives  142 us (46%)
  waiting for transfers between devices  55.9 us (18%)
  matrix products  47.5 us (16%)
  other arithmetic  17.1 us (6%)
  local copies, waits for them, and re-layouts  16.1 us (5%)
  between operations  13.7 us (4%)
  starting transfers between devices  12.8 us (4%)
    all_gather x1, blocking collectives, per_device(): key_piece = lax.all_gather(new_keys, 'ctx', axis=1, tiled=True)  111 us
    all_gather x1, waiting for transfers between devices, per_device(): piece = lax.all_gather(queries, 'ctx', axis=1, tiled=True)  50.3 us
    dot_general x8, matrix products, one_head(): jnp.einsum('sgrc,scd->sgrd', expo, v_head.astype(jnp.float32), precision=...  39.9 us
    all_gather x1, blocking collectives, per_device(): value_piece = lax.all_gather(new_values, 'ctx', axis=1, tiled=True)  30.9 us
    reduce_sum x8, other arithmetic, one_head(): total = jnp.sum(expo, axis=-1)  8.85 us
    dot_general x8, matrix products, one_head(): jnp.einsum('srgd,scd->sgrc', q_head, k_head, preferred_element_type=jnp.f...  6.68 us
    transpose x1, local copies, waits for them, and re-layouts, attend(): jnp.transpose(summed, (1, 3, 0, 2, 4))  6.58 us
  transfers between devices with their start and end apart: 4, of which 2 were waited for; matrix products, arithmetic and copies ran while one was open for 6% of the time, Pallas kernels for 0%

commit v1 on v0

--- a/solution.py
+++ b/solution.py
@@ -64,8 +64,11 @@
     factor = jnp.exp(peaks - hist_top[None])
     hist_total = jnp.sum(totals * factor, axis=0)
     hist_sum = jnp.sum(sums * factor[..., None], axis=0)
-    key_piece = lax.all_gather(new_keys, "ctx", axis=1, tiled=True)
-    value_piece = lax.all_gather(new_values, "ctx", axis=1, tiled=True)
+    key_piece, value_piece = jnp.split(
+        lax.all_gather(jnp.concatenate([new_keys, new_values], axis=0), "ctx", axis=1, tiled=True),
+        [new_keys.shape[0]],
+        axis=0,
+    )
     cols = key_piece.shape[1]
     causal = lax.iota(jnp.int32, cols)[None, :] <= own_ids[:, None]
     visible = causal[None]

time: 306 us -> 276 us (0.902)
  blocking collectives: 142 us -> 112 us
    all_gather x2 -> x1, blocking collectives: 142 us -> 112 us  [per_device(): lax.all_gather(jnp.concatenate([new_keys, new_values], axis=0), 'ctx', ax...]
  transfers between devices with their start and end apart: 4 -> 4, of which waited for: 2 -> 2; matrix products, arithmetic and copies ran while one was open for 6% -> 7% of each run, Pallas kernels for 0% -> 0%
where the time goes in v1:
time: 276 us; the launch traced here: 275 us
  blocking collectives  112 us (41%)
  waiting for transfers between devices  55.9 us (20%)
  matrix products  47.5 us (17%)
  other arithmetic  17.2 us (6%)
  local copies, waits for them, and re-layouts  16.1 us (6%)
  between operations  13.7 us (5%)
  starting transfers between devices  12.8 us (5%)
    all_gather x1, blocking collectives, per_device(): lax.all_gather(jnp.concatenate([new_keys, new_values], axis=0), 'ctx', ax...  112 us
    all_gather x1, waiting for transfers between devices, per_device(): piece = lax.all_gather(queries, 'ctx', axis=1, tiled=True)  50.3 us
    dot_general x8, matrix products, one_head(): jnp.einsum('sgrc,scd->sgrd', expo, v_head.astype(jnp.float32), precision=...  39.9 us
    reduce_sum x8, other arithmetic, one_head(): total = jnp.sum(expo, axis=-1)  8.85 us
    dot_general x8, matrix products, one_head(): jnp.einsum('srgd,scd->sgrc', q_head, k_head, preferred_element_type=jnp.f...  6.68 us
    transpose x1, local copies, waits for them, and re-layouts, attend(): jnp.transpose(summed, (1, 3, 0, 2, 4))  6.58 us
    all_to_all x1, starting transfers between devices, per_device(): lax.all_to_all(summed_all[None], 'ctx', split_axis=2, concat_axis=0, tile...  5.91 us
  transfers between devices with their start and end apart: 4, of which 2 were waited for; matrix products, arithmetic and copies ran while one was open for 7% of the time, Pallas kernels for 0%

profile of v1, /device:TPU:0, one launch (start us, length us, event | category | flops | bytes accessed | tf_op | source)
XLA Modules:
  0.0 275.2 jit_solution(17104726848087387540)
XLA Ops:
  6.5 0.7 all-gather.2.cloned.1.call-update
  7.3 0.9 convolution_compare_fusion
  8.2 2.8 %copy_bitcast_fusion.2 = (bf16[4,1,1024,128]{3,2,1,0:T(8,128)(2,1)}, bf16[4,1,1024,128]{3,2,1,0:T(8,128)(2,1)S(1)}) fusion(bf16[1,1024,4,128]{3,2,1,0:T(4,128)(2,1)} %param.14, bf16[1,1024,4,128]{3,2,1,0:T(4,128)(2,1)} %param.13), kind=kLoop, calls=%fused_computation.58 | loop fusion | bytes 4194304 | tf_op jit(solution)/shard_map/transpose | solution.py:47
  11.0 50.3 %all-gather.2.cloned.1.call-done = bf16[1,256,32,128]{3,2,0,1:T(8,128)(2,1)} async-done(((bf16[1,32,32,128]{3,2,0,1:T(8,128)(2,1)}), bf16[1,256,32,128]{3,2,0,1:T(8,128)(2,1)}) %all-gather.2.cloned.1.call-update) | async-done | bytes 2097168 | tf_op jit(solution)/shard_map/all_gather | solution.py:48
  61.3 2.4 copy.68
  63.7 52.7 %while.30 = (s32[]{:T(128)}, f32[4,1,8,256]{3,2,1,0:T(8,128)S(1)}, f32[4,1,8,256]{3,2,1,0:T(8,128)S(1)}, f32[4,1,8,256,128]{4,3,2,1,0:T(8,128)}, bf16[4,1,1024,1...) while((s32[]{:T(128)}, f32[4,1,8,256]{3,2,1,0:T(8,128)S(1)}, ...), condition=%wide.region_3.4_spmd.clone, body=%wide.region_0.3_spmd.clone.sunk | while | flops 3783258112 | bytes 28381280 | solution.py:33
  63.8 1.4 fusion.77
  65.2 9.6 %fusion.79 = f32[4,1,8,256,128]{4,3,2,1,0:T(8,128)} fusion(f32[4,1,8,256,128]{4,3,2,1,0:T(8,128)} %get-tuple-element.311, s32[]{:T(128)} %get-tuple-element.308, f32[1024,256,8]{1,0,2:T(8,128)S(1)} %get-tuple-element.283, f32[8,256]{1,0:T(8,128)S(1)} %get-tuple-element.284, pred[256,1024]{0,1:T(8,128)(4,1)S(1)} %bitcast.193, ...), kind=kOutput, calls=%fused_computation.14.clone.1 | convolution fusion | flops 3229614080 | bytes 9970688 | tf_op jit(solution)/shard_map/while/body/eval_jaxpr/sgrc,scd->sgrd/dot_general | solution.py:28
  74.8 2.0 fusion.78
  77.0 1.4 fusion.77
  78.4 9.7 %fusion.79 = f32[4,1,8,256,128]{4,3,2,1,0:T(8,128)} fusion(f32[4,1,8,256,128]{4,3,2,1,0:T(8,128)} %get-tuple-element.311, s32[]{:T(128)} %get-tuple-element.308, f32[1024,256,8]{1,0,2:T(8,128)S(1)} %get-tuple-element.283, f32[8,256]{1,0:T(8,128)S(1)} %get-tuple-element.284, pred[256,1024]{0,1:T(8,128)(4,1)S(1)} %bitcast.193, ...), kind=kOutput, calls=%fused_computation.14.clone.1 | convolution fusion | flops 3229614080 | bytes 9970688 | tf_op jit(solution)/shard_map/while/body/eval_jaxpr/sgrc,scd->sgrd/dot_general | solution.py:28
  88.0 2.0 fusion.78
  90.2 1.4 fusion.77
  91.6 9.7 %fusion.79 = f32[4,1,8,256,128]{4,3,2,1,0:T(8,128)} fusion(f32[4,1,8,256,128]{4,3,2,1,0:T(8,128)} %get-tuple-element.311, s32[]{:T(128)} %get-tuple-element.308, f32[1024,256,8]{1,0,2:T(8,128)S(1)} %get-tuple-element.283, f32[8,256]{1,0:T(8,128)S(1)} %get-tuple-element.284, pred[256,1024]{0,1:T(8,128)(4,1)S(1)} %bitcast.193, ...), kind=kOutput, calls=%fused_computation.14.clone.1 | convolution fusion | flops 3229614080 | bytes 9970688 | tf_op jit(solution)/shard_map/while/body/eval_jaxpr/sgrc,scd->sgrd/dot_general | solution.py:28
  101.2 2.0 fusion.78
  103.4 1.4 fusion.77
  104.8 9.6 %fusion.79 = f32[4,1,8,256,128]{4,3,2,1,0:T(8,128)} fusion(f32[4,1,8,256,128]{4,3,2,1,0:T(8,128)} %get-tuple-element.311, s32[]{:T(128)} %get-tuple-element.308, f32[1024,256,8]{1,0,2:T(8,128)S(1)} %get-tuple-element.283, f32[8,256]{1,0:T(8,128)S(1)} %get-tuple-element.284, pred[256,1024]{0,1:T(8,128)(4,1)S(1)} %bitcast.193, ...), kind=kOutput, calls=%fused_computation.14.clone.1 | convolution fusion | flops 3229614080 | bytes 9970688 | tf_op jit(solution)/shard_map/while/body/eval_jaxpr/sgrc,scd->sgrd/dot_general | solution.py:28
  114.4 2.0 fusion.78
  117.1 0.9 reduce.7
  118.0 0.7 reshape.378
  118.8 3.5 %all-to-all-start.1 = ((f32[8,1,1024]{2,1,0:T(1,128)}), f32[8,1,1024]{2,1,0:T(1,128)S(1)}, u32[]{:S(2)}, u32[]{:S(2)}) async-start(f32[8,1,1024]{2,1,0:T(1,128)} %reshape.378), calls=%async_computation.1 | async-start | bytes 65536 | tf_op jit(solution)/shard_map/all_to_all | solution.py:59
  122.4 0.9 reduce.9
  123.4 0.7 reshape.380
  124.1 4.9 %all-to-all-done.1 = f32[8,1,1024]{2,1,0:T(1,128)S(1)} async-done(((f32[8,1,1024]{2,1,0:T(1,128)}), f32[8,1,1024]{2,1,0:T(1,128)S(1)}, u32[]{:S(2)}, u32[]{:S(2)}) %all-to-all-start.1) | async-done | bytes 32800 | tf_op jit(solution)/shard_map/all_to_all | solution.py:59
  128.9 3.3 %all-to-all-start.2 = ((f32[8,1,1024]{2,1,0:T(1,128)}), f32[8,1,1024]{2,1,0:T(1,128)S(1)}, u32[]{:S(2)}, u32[]{:S(2)}) async-start(f32[8,1,1024]{2,1,0:T(1,128)} %reshape.380), calls=%async_computation.2 | async-start | bytes 65536 | tf_op jit(solution)/shard_map/all_to_all | solution.py:60
  132.3 6.6 %copy.67 = f32[1,256,4,8,128]{4,3,2,1,0:T(8,128)} copy(f32[1,256,4,8,128]{4,1,3,0,2:T(8,128)} %bitcast.197) | data formatting | bytes 8388608 | tf_op jit(solution)/shard_map/transpose | solution.py:36
  138.9 5.9 %all-to-all-start = ((f32[1,1,256,32,128]{4,3,1,0,2:T(8,128)}), f32[1,1,256,32,128]{4,3,1,0,2:T(8,128)}, u32[]{:S(2)}, u32[]{:S(2)}) async-start(f32[1,1,256,32,128]{4,3,1,0,2:T(8,128)} %bitcast.195), calls=%async_computation | async-start | bytes 8388608 | tf_op jit(solution)/shard_map/all_to_all | solution.py:61
  145.0 111.7 %all_gather.7 = bf16[2,256,4,128]{3,1,0,2:T(8,128)(2,1)S(1)} all-gather(bf16[2,32,4,128]{3,1,0,2:T(8,128)(2,1)S(1)} %pad_maximum_fusion), channel_id=1, replica_groups=mesh['groups'=2,'ctx'=8,'head'=2] {'ctx'}, dimensions={1}, use_global_device_ids=true | all-gather | bytes 589824 | tf_op jit(solution)/shard_map/all_gather | solution.py:68
  256.8 3.7 %while.31 = (s32[]{:T(128)}, f32[4,1,8,32]{3,2,1,0:T(8,128)S(1)}, f32[4,1,8,32]{3,2,1,0:T(8,128)S(1)}, f32[4,1,8,32,128]{4,3,2,1,0:T(8,128)S(1)}, bf16[4,1,256,1...) while((s32[]{:T(128)}, f32[4,1,8,32]{3,2,1,0:T(8,128)S(1)}, ...), condition=%wide.region_9.10_spmd.clone, body=%wide.region_6.9_spmd.clone.sunk | while | flops 117972480 | bytes 1172705 | solution.py:33
  261.7 0.7 reduce.10
  263.0 3.9 %fusion.49 = f32[32,32,128]{2,0,1:T(8,128)S(1)} fusion(f32[8,1,32,32,128]{4,3,2,0,1:T(8,128)} %bitcast.8, f32[8,32,32]{1,0,2:T(8,128)S(1)} %copy.48), kind=kLoop, calls=%fused_computation.54 | loop fusion | flops 1966080 | bytes 4751360 | tf_op jit(solution)/shard_map/reduce_sum | solution.py:66
  267.5 0.8 copy.57
  (65 shorter events, 7.1 us)
Async XLA Ops:
  6.5 54.8 %all-gather.2.cloned.1.call-start = ((), (), s32[]{:S(2)}) async-start(), calls=%async_computation.3 | async-start | bytes 2359296 | tf_op jit(solution)/shard_map/all_gather | solution.py:48
  118.8 10.2 %all-to-all-start.1 = ((f32[8,1,1024]{2,1,0:T(1,128)}), f32[8,1,1024]{2,1,0:T(1,128)S(1)}, u32[]{:S(2)}, u32[]{:S(2)}) async-start(f32[8,1,1024]{2,1,0:T(1,128)} %reshape.378), calls=%async_computation.1 | async-start | bytes 65536 | tf_op jit(solution)/shard_map/all_to_all | solution.py:59
  128.9 10.0 %all-to-all-start.2 = ((f32[8,1,1024]{2,1,0:T(1,128)}), f32[8,1,1024]{2,1,0:T(1,128)S(1)}, u32[]{:S(2)}, u32[]{:S(2)}) async-start(f32[8,1,1024]{2,1,0:T(1,128)} %reshape.380), calls=%async_computation.2 | async-start | bytes 65536 | tf_op jit(solution)/shard_map/all_to_all | solution.py:60
  132.3 12.5 %copy-start = (bf16[1,32,32,128]{3,2,1,0:T(8,128)(2,1)S(1)}, bf16[1,32,32,128]{3,2,1,0:T(8,128)(2,1)}, u32[]{:S(2)}) copy-start(bf16[1,32,32,128]{3,2,1,0:T(8,128)(2,1)} %param.10) | copy-start | bytes 786436
  132.3 12.7 %copy-start.1 = (bf16[1,32,4,128]{3,2,1,0:T(4,128)(2,1)S(1)}, bf16[1,32,4,128]{3,2,1,0:T(4,128)(2,1)}, u32[]{:S(2)}) copy-start(bf16[1,32,4,128]{3,2,1,0:T(4,128)(2,1)} %param.11) | copy-start | bytes 98308
  132.3 12.7 %copy-start.2 = (bf16[1,32,4,128]{3,2,1,0:T(4,128)(2,1)S(1)}, bf16[1,32,4,128]{3,2,1,0:T(4,128)(2,1)}, u32[]{:S(2)}) copy-start(bf16[1,32,4,128]{3,2,1,0:T(4,128)(2,1)} %param.12) | copy-start | bytes 98308
  138.9 124.1 %all-to-all-start = ((f32[1,1,256,32,128]{4,3,1,0,2:T(8,128)}), f32[1,1,256,32,128]{4,3,1,0,2:T(8,128)}, u32[]{:S(2)}, u32[]{:S(2)}) async-start(f32[1,1,256,32,128]{4,3,1,0,2:T(8,128)} %bitcast.195), calls=%async_computation | async-start | bytes 8388608 | tf_op jit(solution)/shard_map/all_to_all | solution.py:61
Sparse Core Ops, SparseCore 0:
  9.5 51.8 all-gather.1
